TPU v7x, 256 devices: a whole 4x4x8 slice. The times are simulated.
256 devices in a mesh: comp: 2 (over core), gx: 8 (over y, z_lo), gy: 16 (over x, z_hi).
Axes of the slice: x: 4, y: 4, z: 8 (z_hi: 4, z_lo: 2; z = z_hi * 2 + z_lo), core: 2. Of those that a mesh axis runs over, the one named last changes fastest.
Arguments:
- state_incr: float32 [2, 2, 128, 128, 2048], P('comp', None, None, 'gx', 'gy'), may hold values from -6 to 6
- winds: float32 [2, 2, 128, 128, 2048], P('comp', None, None, 'gx', 'gy'), may hold values from -0.4 to 0.4
- coupling: float32 [128, 2048], P('gx', 'gy'), may hold values from 0.1 to 0.6
- background: float32 [2, 2, 128], P('comp'), may hold values from 0.5 to 2
- obs_dest: int32 [131072, 1], P(('comp', 'gx', 'gy')), may hold values from 0 to 127; in each aligned block of 512 rows (0 to 511, 512 to 1023, ...) at most 8 rows name the same one
- obs_col: int32 [131072], P(('comp', 'gx', 'gy')), may hold values from 0 to 2047
- obs_op: float32 [131072, 256], P(('comp', 'gx', 'gy')), may hold values from -0.375 to 0.375
- obs_prec: float32 [131072], P(('comp', 'gx', 'gy')), may hold values from 0.5 to 4
Outputs:
- hess_vec: float32 [2, 2, 128, 128, 2048], P('comp', None, None, 'gx', 'gy')
Inputs may be any that keep to these rules, and one draw needn't show every extreme that they name: `obs_dest`: among the rows of one device at most 8 name the same owner, a bound that some block reaches of them; owners are tiles of the record's own component. `obs_col`: column m of a tile is its cell (m // 128, m % 128).
All inputs are finite; a program needn't handle non-finite values.
Results may differ from a plain program's by a relative error of at most 0.000057.
Values sent between devices are 32-bit elements; how exact they have to be, the bound alone decides.
A program may use at most 128 MiB of HBM per device.

v0:
```python
import jax
import jax.numpy as jnp
from jax import lax
from jax.experimental import pallas as pl
from jax.experimental.pallas import tpu as pltpu
from jax.sharding import PartitionSpec as P

MESH = pl.DeviceIdType.MESH
F32 = jnp.float32
BF16 = jnp.bfloat16
CHUNKS = 4
GROUP = 32


def coordinates(gx, gy):
    return gy // 4, gx // 2, (gy % 4) * 2 + gx % 2


def device(x, y, z):
    return {"gx": y * 2 + z % 2, "gy": x * 4 + z // 2}


def split(value):
    high = value.astype(BF16)
    return high, (value - high.astype(F32)).astype(BF16)


def matmul(a, b):
    return lax.dot_general(a, b, (((1,), (0,)), ((), ())), preferred_element_type=F32)


def matmul_nt(a, b):
    return lax.dot_general(a, b, (((1,), (1,)), ((), ())), preferred_element_type=F32)


def kernel(
    state_hbm, winds_hbm, op_hbm, meta_ref, gamma_ref, out_hbm,
    cells, spare, winds, ops, send, recv,
    row_out, row_in, lane_out, lane_in, top_out, top_in,
    second_hi, second_lo, select,
    load_sem, op_sem, store_sem, a2a_send, a2a_recv, halo_send, halo_recv, top_send, top_recv, plane_sem, line_sem,
):
    comp = lax.axis_index("comp")
    gx = lax.axis_index("gx")
    gy = lax.axis_index("gy")
    x, y, z = coordinates(gx, gy)
    levels = 128

    load_state = pltpu.make_async_copy(state_hbm, cells, load_sem.at[0])
    load_winds = pltpu.make_async_copy(winds_hbm, winds, load_sem.at[1])
    load_ops = pltpu.make_async_copy(op_hbm, ops, op_sem)
    load_state.start()
    load_ops.start()
    load_winds.start()

    neighbours = (
        {"gx": (gx + 1) % 8},
        {"gx": (gx + 7) % 8},
        {"gy": (gy + 1) % 16},
        {"gy": (gy + 15) % 16},
    )
    partner = {"comp": 1 - comp}

    barrier = pltpu.get_barrier_semaphore()

    def greet(semaphore, target):
        pl.semaphore_signal(semaphore, inc=1, device_id=target, device_id_type=MESH)

    greet(barrier, partner)
    for target in neighbours:
        greet(barrier, target)
    for step in range(1, 4):
        greet(barrier, device((x + step) % 4, y, z))
    for step in range(1, 4):
        greet(barrier, device(x, (y + step) % 4, z))
    for step in range(1, 8):
        greet(barrier, device(x, y, (z + step) % 8))

    row = lax.broadcasted_iota(jnp.int32, (16, 128), 0)
    lane = lax.broadcasted_iota(jnp.int32, (16, 128), 1)
    has_low = jnp.where(gx > 0, 1.0, 0.0)
    has_high = jnp.where(gx < 7, 1.0, 0.0)
    has_left = jnp.where(gy > 0, 1.0, 0.0)
    has_right = jnp.where(gy < 15, 1.0, 0.0)
    gamma = gamma_ref[...]
    own_share = jnp.where(comp == 0, 1.0, 0.5)
    peer_share = 1.5 - own_share

    def halo_copies(sweep):
        pairs = (
            (row_out.at[sweep, 0], row_in.at[sweep, 0]),
            (row_out.at[sweep, 1], row_in.at[sweep, 1]),
            (lane_out.at[sweep, 0], lane_in.at[sweep, 0]),
            (lane_out.at[sweep, 1], lane_in.at[sweep, 1]),
        )
        return [
            pltpu.make_async_remote_copy(
                src, dst, halo_send.at[sweep, n], halo_recv.at[sweep, n],
                device_id=neighbours[n], device_id_type=MESH,
            )
            for n, (src, dst) in enumerate(pairs)
        ]

    def top_copy(sweep):
        return pltpu.make_async_remote_copy(
            top_out.at[sweep], top_in.at[sweep], top_send.at[sweep], top_recv.at[sweep],
            device_id=partner, device_id_type=MESH,
        )

    def keep_edges(sweep, fk, k, up, down, right, left, f, carry):
        row_out[sweep, 0, pl.ds(fk, 1), :] = up[15:16]
        row_out[sweep, 1, pl.ds(fk, 1), :] = down[0:1]
        here = lane == k
        rights = jnp.where(here, jnp.broadcast_to(right[:, 127:128], (16, 128)), carry[2 * f])
        lefts = jnp.where(here, jnp.broadcast_to(left[:, 0:1], (16, 128)), carry[2 * f + 1])
        return carry[: 2 * f] + (rights, lefts) + carry[2 * f + 2 :]

    def store_lanes(sweep, carry):
        for f in range(2):
            lane_out[sweep, 0, 16 * f : 16 * f + 16, :] = carry[2 * f]
            lane_out[sweep, 1, 16 * f : 16 * f + 16, :] = carry[2 * f + 1]

    def halos(sweep, fk, f, k):
        low = row_in[sweep, 0, pl.ds(fk, 1), :] * has_low
        high = row_in[sweep, 1, pl.ds(fk, 1), :] * has_high
        left = pltpu.roll(lane_in[sweep, 0, 16 * f : 16 * f + 16, :], (128 - k) % 128, 1) * has_left
        right = pltpu.roll(lane_in[sweep, 1, 16 * f : 16 * f + 16, :], 127 - k, 1) * has_right
        return low, high, left, right

    blank = jnp.zeros((16, 128), F32)

    load_state.wait()

    def raw_edges(k, carry):
        for f in range(2):
            fk = f * levels + k
            value = cells[fk]
            carry = keep_edges(0, fk, k, value, value, value, value, f, carry)
        return carry

    store_lanes(0, lax.fori_loop(0, levels, raw_edges, (blank,) * 4, unroll=4))
    pl.semaphore_wait(barrier, 18)
    first_halo = halo_copies(0)
    for copy in first_halo:
        copy.start()
    for step in range(1, 4):
        greet(plane_sem, device(x, (y + step) % 4, z))

    load_ops.wait()
    owner = meta_ref[0:1, :].astype(jnp.int32)
    owner_gx, owner_gy = owner // 16, owner % 16
    owner_x, owner_y, owner_z = owner_gy // 4, owner_gx // 2, (owner_gy % 4) * 2 + owner_gx % 2
    relative = ((owner_y - y + 4) % 4) * 32 + ((owner_x - x + 4) % 4) * 8 + (owner_z - z + 8) % 8
    tile_iota = lax.broadcasted_iota(jnp.int32, (128, 512), 0)
    hits = jnp.where(tile_iota == relative, 1.0, 0.0)
    hits_narrow = hits.astype(BF16)
    earlier = jnp.where(
        lax.broadcasted_iota(jnp.int32, (512, 512), 0) < lax.broadcasted_iota(jnp.int32, (512, 512), 1), 1.0, 0.0
    ).astype(BF16)
    slot = jnp.sum(matmul(hits_narrow, earlier) * hits, axis=0, keepdims=True).astype(jnp.int32)
    position = relative * 8 + slot
    column = meta_ref[1:2, :].astype(jnp.int32)
    in_row = tile_iota == (relative % 16) * 8 + slot
    column_high = jnp.where(in_row, (column // 128).astype(F32), 0.0).astype(BF16)
    column_low = jnp.where(in_row, (column % 128).astype(F32), 0.0).astype(BF16)
    columns = 128.0 * matmul_nt(hits_narrow, column_high) + matmul_nt(hits_narrow, column_low)
    send[:, 16, :] = columns
    scale_high, scale_low = split(jnp.broadcast_to(jnp.sqrt(meta_ref[2:3, :]), (128, 512)))
    ops_high, ops_low = split(ops[...])

    def pack(chunk, _):
        slots = lax.broadcasted_iota(jnp.int32, (256, 512), 0) + chunk * 256
        pick = jnp.where(slots == position, 1.0, 0.0).astype(BF16)
        scale = matmul_nt(pick, scale_high) + matmul_nt(pick, scale_low)
        rows = matmul(pick, ops_high) + matmul(pick, ops_low)
        target = pl.ds(chunk * GROUP, GROUP)
        send[target, 0:8, :] = (rows[:, :128] * scale).reshape(GROUP, 8, 128)
        send[target, 8:16, :] = (rows[:, 128:] * scale).reshape(GROUP, 8, 128)
        return 0

    lax.fori_loop(0, CHUNKS, pack, 0)
    pl.semaphore_wait(plane_sem, 3)
    for step in range(1, 8):
        greet(line_sem, device(x, y, (z + step) % 8))
    pl.semaphore_wait(line_sem, 7)

    pltpu.make_async_copy(send.at[0], recv.at[0], a2a_recv.at[0]).start()

    def dispatch(s, _):
        target = device((x + (s // 8) % 4) % 4, (y + s // 32) % 4, (z + s % 8) % 8)
        pltpu.make_async_remote_copy(
            send.at[s], recv.at[s], a2a_send, a2a_recv.at[s // GROUP],
            device_id=target, device_id_type=MESH,
        ).start()
        return 0

    lax.fori_loop(1, 128, dispatch, 0)

    load_winds.wait()

    def forward(sweep, source, target, last):
        def level(k, carry):
            wind_x = winds[k]
            wind_y = winds[levels + k]
            for f in range(2):
                fk = f * levels + k
                here = source[fk]
                above = source[f * levels + jnp.minimum(k + 1, levels - 1)]
                below = source[f * levels + jnp.maximum(k - 1, 0)]
                low, high, left, right = halos(sweep, fk, f, k)
                up = jnp.where(row == 15, high, pltpu.roll(here, 15, 0))
                down = jnp.where(row == 0, low, pltpu.roll(here, 1, 0))
                east = jnp.where(lane == 127, right, pltpu.roll(here, 127, 1))
                west = jnp.where(lane == 0, left, pltpu.roll(here, 1, 1))
                value = (
                    0.3 * here + 0.15 * (above + below) + 0.1 * ((up + down) + (east + west))
                    - 0.5 * (wind_x * (up - down) + wind_y * (east - west))
                )
                target[fk] = value
                if not last:
                    carry = keep_edges(sweep + 1, fk, k, value, value, value, value, f, carry)
            return carry

        level(0, (blank,) * 4)
        for f in range(2):
            top_out[sweep, 16 * f : 16 * f + 16, :] = target[f * levels]
        copy = top_copy(sweep)
        copy.start()
        carry = lax.fori_loop(1, levels, level, (blank,) * 4, unroll=4)
        copy.wait_recv()
        for f in range(2):
            own = target[f * levels]
            value = own - own_share * gamma * (own - top_in[sweep, 16 * f : 16 * f + 16, :])
            target[f * levels] = value
            if not last:
                carry = keep_edges(sweep + 1, f * levels, 0, value, value, value, value, f, carry)
        if not last:
            store_lanes(sweep + 1, carry)
        return copy

    for copy in first_halo:
        copy.wait_recv()
    first_top = forward(0, cells, spare, False)
    second_halo = halo_copies(1)
    for copy in second_halo:
        copy.start()
    for copy in second_halo:
        copy.wait_recv()
    second_top = forward(1, spare, cells, True)

    flat_cells = cells.reshape(256 * 16, 128)
    for i in range(16):
        high, low = split(flat_cells[pl.ds(i, 256, stride=16), :])
        second_hi[:, 128 * i : 128 * i + 128] = high
        second_lo[:, 128 * i : 128 * i + 128] = low

    def clear(fk, _):
        spare[fk] = blank
        return 0

    lax.fori_loop(0, 256, clear, 0, unroll=8)
    flat_spare = spare.reshape(256 * 16, 128)

    def observe(chunk, _):
        arrived = recv.at[pl.ds(chunk * GROUP, GROUP)]
        pltpu.make_async_copy(arrived, arrived, a2a_recv.at[chunk]).wait()
        first = pl.ds(chunk * GROUP, 16)
        other = pl.ds(chunk * GROUP + 16, 16)
        where = jnp.concatenate(
            [jnp.sum(recv[first, 16, :], axis=0, keepdims=True), jnp.sum(recv[other, 16, :], axis=0, keepdims=True)],
            axis=1,
        ).astype(jnp.int32)
        for part in range(8):
            cell = lax.broadcasted_iota(jnp.int32, (256, 256), 0) + 256 * part
            select[256 * part : 256 * part + 256, :] = jnp.where(cell == where, 1.0, 0.0).astype(BF16)
        group = pl.ds(chunk * GROUP, GROUP)
        weights = jnp.concatenate(
            [recv[group, 0:8, :].reshape(256, 128).T, recv[group, 8:16, :].reshape(256, 128).T], axis=0
        )
        sampled = matmul(second_hi[...], select[...]) + matmul(second_lo[...], select[...])
        innovation = jnp.sum(sampled * weights, axis=0, keepdims=True)
        spread_high, spread_low = split(weights * innovation)
        for i in range(16):
            cells_of_row = select[128 * i : 128 * i + 128, :]
            flat_spare[pl.ds(i, 256, stride=16), :] += matmul_nt(spread_high, cells_of_row) + matmul_nt(
                spread_low, cells_of_row
            )
        return 0

    lax.fori_loop(0, CHUNKS, observe, 0)

    def adjoint(sweep, source, target, last):
        for f in range(2):
            top_out[sweep, 16 * f : 16 * f + 16, :] = source[f * levels]
        top = top_copy(sweep)
        top.start()

        def parts(fk, k):
            here = source[fk]
            even = 0.1 * here
            along_x = 0.5 * winds[k] * here
            along_y = 0.5 * winds[levels + k] * here
            return here, even - along_x, even + along_x, even - along_y, even + along_y

        def edges(k, carry):
            for f in range(2):
                fk = f * levels + k
                _, up, down, right, left = parts(fk, k)
                carry = keep_edges(sweep, fk, k, up, down, right, left, f, carry)
            return carry

        carry = lax.fori_loop(1, levels, edges, (blank,) * 4, unroll=4)
        top.wait_recv()
        for f in range(2):
            own = source[f * levels]
            source[f * levels] = (
                own - own_share * gamma * own + peer_share * gamma * top_in[sweep, 16 * f : 16 * f + 16, :]
            )
        store_lanes(sweep, edges(0, carry))
        copies = halo_copies(sweep)
        for copy in copies:
            copy.start()

        def inside(k, _):
            for f in range(2):
                fk = f * levels + k
                here, up, down, right, left = parts(fk, k)
                above = source[f * levels + jnp.minimum(k + 1, levels - 1)]
                below = source[f * levels + jnp.maximum(k - 1, 0)]
                target[fk] = (
                    0.3 * here + 0.15 * (above + below)
                    + jnp.where(row == 0, 0.0, pltpu.roll(up, 1, 0))
                    + jnp.where(row == 15, 0.0, pltpu.roll(down, 15, 0))
                    + jnp.where(lane == 0, 0.0, pltpu.roll(right, 1, 1))
                    + jnp.where(lane == 127, 0.0, pltpu.roll(left, 127, 1))
                )
            return 0

        lax.fori_loop(0, levels, inside, 0, unroll=4)
        for copy in copies:
            copy.wait_recv()

        def outside(k, _):
            for f in range(2):
                fk = f * levels + k
                low, high, left, right = halos(sweep, fk, f, k)
                target[fk] = (
                    target[fk]
                    + jnp.where(row == 0, low, 0.0) + jnp.where(row == 15, high, 0.0)
                    + jnp.where(lane == 0, left, 0.0) + jnp.where(lane == 127, right, 0.0)
                )
            return 0

        lax.fori_loop(0, levels, outside, 0, unroll=4)
        return [top] + copies

    started = [first_top, second_top] + first_halo + second_halo
    started += adjoint(2, spare, cells, False)
    started += adjoint(3, cells, spare, True)
    store = pltpu.make_async_copy(spare, out_hbm, store_sem)
    store.start()
    for copy in started:
        copy.wait_send()
    sent = recv.at[pl.ds(1, 127)]
    pltpu.make_async_copy(sent, sent, a2a_send).wait()
    store.wait()


def local(state_incr, winds, coupling, background, obs_dest, obs_col, obs_op, obs_prec):
    shape = state_incr.shape[1:]
    slabs = shape[0] * shape[1]
    meta = jnp.stack([obs_dest[:, 0].astype(F32), obs_col.astype(F32), obs_prec])
    hbm = pl.BlockSpec(memory_space=pl.ANY)
    vmem = pl.BlockSpec(memory_space=pltpu.VMEM)
    tile = (slabs,) + shape[2:]
    adjoint = pl.pallas_call(
        kernel,
        out_shape=jax.ShapeDtypeStruct(tile, F32),
        in_specs=[hbm, hbm, hbm, vmem, vmem],
        out_specs=hbm,
        scratch_shapes=[
            pltpu.VMEM(tile, F32),
            pltpu.VMEM(tile, F32),
            pltpu.VMEM(tile, F32),
            pltpu.VMEM((512, 256), F32),
            pltpu.VMEM((128, 17, 128), F32),
            pltpu.VMEM((128, 17, 128), F32),
            pltpu.VMEM((4, 2, 256, 128), F32),
            pltpu.VMEM((4, 2, 256, 128), F32),
            pltpu.VMEM((4, 2, 32, 128), F32),
            pltpu.VMEM((4, 2, 32, 128), F32),
            pltpu.VMEM((4, 32, 128), F32),
            pltpu.VMEM((4, 32, 128), F32),
            pltpu.VMEM((256, 2048), BF16),
            pltpu.VMEM((256, 2048), BF16),
            pltpu.VMEM((2048, 256), BF16),
            pltpu.SemaphoreType.DMA((2,)),
            pltpu.SemaphoreType.DMA,
            pltpu.SemaphoreType.DMA,
            pltpu.SemaphoreType.DMA,
            pltpu.SemaphoreType.DMA((CHUNKS,)),
            pltpu.SemaphoreType.DMA((4, 4)),
            pltpu.SemaphoreType.DMA((4, 4)),
            pltpu.SemaphoreType.DMA((4,)),
            pltpu.SemaphoreType.DMA((4,)),
            pltpu.SemaphoreType.REGULAR,
            pltpu.SemaphoreType.REGULAR,
        ],
        compiler_params=pltpu.CompilerParams(
            collective_id=0, has_side_effects=True, vmem_limit_bytes=56 * 1024 * 1024
        ),
    )(state_incr.reshape(tile), winds.reshape(tile), obs_op, meta, coupling)
    result = background[0][:, :, None, None] * state_incr[0] + adjoint.reshape(shape)
    return result[None]


def solution(mesh):
    placed = (
        P("comp", None, None, "gx", "gy"),
        P("comp", None, None, "gx", "gy"),
        P("gx", "gy"),
        P("comp", None, None),
        P(("comp", "gx", "gy"), None),
        P(("comp", "gx", "gy")),
        P(("comp", "gx", "gy"), None),
        P(("comp", "gx", "gy")),
    )
    return jax.shard_map(
        local,
        mesh=mesh,
        in_specs=placed,
        out_specs=P("comp", None, None, "gx", "gy"),
        check_vma=False,
    )
```

profile of v0, /device:TPU:1, one launch (start us, length us, event | category | flops | bytes accessed | tf_op | source)
XLA Modules:
  0.0 108.0 jit_solution(11247427863381763785)
XLA Ops:
  0.0 0.7 convert_bitcast_fusion
  0.7 0.7 convert_element_type.18
  1.4 1.3 %pad_maximum_fusion.meta_ref = f32[3,512]{1,0:T(4,128)} fusion(f32[1,512]{1,0:T(1,128)} %bitcast.12, f32[1,512]{1,0:T(1,128)S(1)} %bitcast.11, f32[1,512]{1,0:T(1,128)S(1)} %convert_bitcast_fusion), kind=kLoop, calls=%fused_computation.1 | loop fusion | flops 3072 | bytes 12288 | tf_op jit(solution)/shard_map/stack | solution.py:372
  2.7 0.0 copy-start
  2.7 0.0 copy-start.1
  2.7 102.0 %shard_map.82 = f32[256,16,128]{2,1,0:T(8,128)} custom-call(f32[256,16,128]{2,1,0:T(8,128)} %bitcast.8, f32[256,16,128]{2,1,0:T(8,128)} %bitcast.10, f32[512,256]{1,0:T(8,128)} %op_hbm.1, f32[3,512]{1,0:T(4,128)} %pad_maximum_fusion.meta_ref, f32[16,128]{1,0:T(8,128)} %gamma_ref.1), custom_call_target="tpu_custom_call" | custom-call | tf_op jit(solution)/shard_map/pallas_call | solution.py:376
  104.7 0.0 copy-done
  104.7 0.0 copy-done.1
  104.7 3.2 %multiply_add_fusion = f32[1,2,128,16,128]{4,3,2,1,0:T(8,128)} fusion(f32[1,2,128,16,128]{4,3,2,1,0:T(8,128)} %bitcast.9, f32[1,2,128,16,128]{4,3,2,1,0:T(8,128)S(1)} %copy-done, f32[2,128]{1,0:T(2,128)S(1)} %bitcast.13), kind=kLoop, calls=%fused_computation | loop fusion | flops 1048576 | bytes 6292480 | tf_op jit(solution)/shard_map/add | solution.py:413
Async XLA Ops:
  2.7 102.0 %copy-start = (f32[1,2,128,16,128]{4,3,2,1,0:T(8,128)S(1)}, f32[1,2,128,16,128]{4,3,2,1,0:T(8,128)}, u32[]{:S(2)}) copy-start(f32[1,2,128,16,128]{4,3,2,1,0:T(8,128)} %param.8) | copy-start | bytes 6291460
  2.7 102.0 %copy-start.1 = (f32[1,2,128]{2,1,0:T(2,128)S(1)}, f32[1,2,128]{2,1,0:T(2,128)}, u32[]{:S(2)}) copy-start(f32[1,2,128]{2,1,0:T(2,128)} %param.11) | copy-start | bytes 3076
where the time goes:
time: 109 us; the launch traced here: 108 us
  Pallas kernels  102 us (94%)
  other arithmetic  5.9 us (5%)
    pallas_call x1, Pallas kernels, local(): pl.pallas_call(kernel, out_shape=jax.ShapeDtypeStruct(tile, F32), in_spec...  102 us
    add x1, other arithmetic, local(): background[0][:, :, None, None] * state_incr[0] + adjoint.reshape(shape)  3.25 us

commit v1 on v0

v1 whole, which is shorter than its diff:
```python
import jax
import jax.numpy as jnp
from jax import lax
from jax.experimental import pallas as pl
from jax.experimental.pallas import tpu as pltpu
from jax.sharding import PartitionSpec as P

MESH = pl.DeviceIdType.MESH
F32 = jnp.float32
BF16 = jnp.bfloat16
CHUNKS = 4
GROUP = 32
PAD = 144
BLOCK = 32


def device(x, y, z):
    return {"gx": y * 2 + (z & 1), "gy": x * 4 + (z >> 1)}


def split(value):
    high = value.astype(BF16)
    return high, (value - high.astype(F32)).astype(BF16)


def matmul(a, b):
    return lax.dot_general(a, b, (((1,), (0,)), ((), ())), preferred_element_type=F32)


def matmul_nt(a, b):
    return lax.dot_general(a, b, (((1,), (1,)), ((), ())), preferred_element_type=F32)


def kernel(
    state_hbm, winds_hbm, op_hbm, owner_hbm, column_hbm, prec_hbm, gamma_hbm, out_hbm,
    owner_ref, column_ref, prec_ref, gamma_ref, native, native_winds, field_0, field_1, field_2, field_3, wind_x, wind_y, exchange, ops, send, recv,
    row_out, lane_out, lane_in, top_out, top_in,
    second, pick_cell,
    load_sem, store_sem, a2a_send, a2a_recv, halo_send, halo_recv, top_send, top_recv, line_sem,
):
    comp = lax.axis_index("comp")
    gx = lax.axis_index("gx")
    gy = lax.axis_index("gy")
    x, y, z = gy >> 2, gx >> 1, ((gy & 3) << 1) | (gx & 1)

    loads = [
        pltpu.make_async_copy(src, dst, load_sem.at[n])
        for n, (src, dst) in enumerate(
            (
                (owner_hbm, owner_ref), (column_hbm, column_ref), (prec_hbm, prec_ref), (op_hbm, ops),
                (state_hbm, native), (winds_hbm, native_winds), (gamma_hbm, gamma_ref),
            )
        )
    ]
    for load in loads:
        load.start()

    neighbours = (
        {"gx": (gx + 1) & 7},
        {"gx": (gx + 7) & 7},
        {"gy": (gy + 1) & 15},
        {"gy": (gy + 15) & 15},
    )
    partner = {"comp": 1 - comp}
    barrier = pltpu.get_barrier_semaphore()

    def greet(semaphore, target):
        pl.semaphore_signal(semaphore, inc=1, device_id=target, device_id_type=MESH)

    for target in neighbours:
        greet(barrier, target)
    greet(barrier, partner)
    for step in range(1, 8):
        greet(barrier, device(x, y, (z + step) & 7))
    for step in range(1, 16):
        greet(barrier, device((x + step) & 3, (y + step // 4) & 3, z))

    lane = lax.broadcasted_iota(jnp.int32, (BLOCK, 128), 1)
    lane_8 = lax.broadcasted_iota(jnp.int32, (8, 128), 1)
    has_left = jnp.where(gy > 0, 1.0, 0.0)
    has_right = jnp.where(gy < 15, 1.0, 0.0)
    own_share = jnp.where(comp == 0, 1.0, 0.5)
    peer_share = 1.5 - own_share
    fields = (field_0, field_1, field_2, field_3)
    flat_fields = [field.reshape(2 * 18 * PAD, 128) for field in fields]
    flat_native = native.reshape(4096, 128)
    flat_winds = native_winds.reshape(4096, 128)
    flat_wind_y = wind_y.reshape(16 * PAD, 128)

    def edge_row(f, j):
        return pl.ds((f * 18 + 1) * PAD + 8 + j, 16, stride=PAD)

    def halo_copies(sweep, sources):
        pairs = (
            (sources[0], fields[sweep].at[:, 0, pl.ds(8, 128), :]),
            (sources[1], fields[sweep].at[:, 17, pl.ds(8, 128), :]),
            (lane_out.at[sweep, 0], lane_in.at[sweep, 0]),
            (lane_out.at[sweep, 1], lane_in.at[sweep, 1]),
        )
        return [
            pltpu.make_async_remote_copy(
                src, dst, halo_send.at[sweep, n], halo_recv.at[sweep, n],
                device_id=neighbours[n], device_id_type=MESH,
            )
            for n, (src, dst) in enumerate(pairs)
        ]

    def start_tangent_halo(sweep):
        copies = halo_copies(
            sweep, (fields[sweep].at[:, 16, pl.ds(8, 128), :], fields[sweep].at[:, 1, pl.ds(8, 128), :])
        )
        copies[0].start()
        copies[1].start()
        for f in range(2):
            lane_out[sweep, 0, 16 * f : 16 * f + 16, :] = flat_fields[sweep][edge_row(f, 127), :]
            lane_out[sweep, 1, 16 * f : 16 * f + 16, :] = flat_fields[sweep][edge_row(f, 0), :]
        copies[2].start()
        copies[3].start()
        return copies

    def take_lanes(sweep, copies):
        copies[2].wait_recv()
        copies[3].wait_recv()
        for f in range(2):
            flat_fields[sweep][edge_row(f, -1), :] = lane_in[sweep, 0, 16 * f : 16 * f + 16, :] * has_left
            flat_fields[sweep][edge_row(f, 128), :] = lane_in[sweep, 1, 16 * f : 16 * f + 16, :] * has_right

    def take_rows(sweep, copies):
        copies[0].wait_recv()
        copies[1].wait_recv()

        @pl.when(gx == 0)
        def _():
            fields[sweep][:, 0, 8:136, :] = jnp.zeros((2, 128, 128), F32)

        @pl.when(gx == 7)
        def _():
            fields[sweep][:, 17, 8:136, :] = jnp.zeros((2, 128, 128), F32)

    def pack_top(sweep, part, field, i):
        for f in range(2):
            rows = pl.ds(f * 16 + (i >> 3) * 8, 8)
            packed = top_out[sweep, part, rows, :]
            base = (i & 7) * 16
            for n in range(16):
                level = fields[field][f, i + 1, 8 + 8 * n : 16 + 8 * n, 0:1]
                packed = jnp.where(lane_8 == base + n, jnp.broadcast_to(level, (8, 128)), packed)
            top_out[sweep, part, rows, :] = packed

    def top_copy(sweep, part):
        return pltpu.make_async_remote_copy(
            top_out.at[sweep, part], top_in.at[sweep, part], top_send.at[sweep, part], top_recv.at[sweep, part],
            device_id=partner, device_id_type=MESH,
        )

    def couple(sweep, part, field, i, transposed):
        for f in range(2):
            rows = pl.ds(f * 16 + (i >> 3) * 8, 8)
            packed = pltpu.roll(top_in[sweep, part, rows, :], (128 - (i & 7) * 16) & 127, 1)
            for half in range(2):
                low = 8 + 64 * half
                own = fields[field][f, i + 1, low : low + 64, :]
                peer = jnp.concatenate(
                    [packed if n == 0 else pltpu.roll(packed, 128 - n, 1) for n in range(8 * half, 8 * half + 8)], axis=0
                )
                rate = exchange[i, 64 * half : 64 * half + 64, :]
                if transposed:
                    value = own - rate * (own_share * own - peer_share * peer)
                else:
                    value = own - rate * (own_share * (own - peer))
                fields[field][f, i + 1, low : low + 64, :] = value

    def vertical(here):
        above = jnp.where(lane == 127, here, pltpu.roll(here, 127, 1))
        below = jnp.where(lane == 0, here, pltpu.roll(here, 1, 1))
        return 0.3 * here + 0.15 * (above + below)

    def neighbourhood(field, f, i, low):
        here = field[f, i + 1, low : low + BLOCK, :]
        up = field[f, i + 2, low : low + BLOCK, :]
        down = field[f, i, low : low + BLOCK, :]
        right = field[f, i + 1, low + 1 : low + 1 + BLOCK, :]
        left = field[f, i + 1, low - 1 : low - 1 + BLOCK, :]
        return here, up, down, right, left

    def tangent_row(sweep, target, i):
        for block in range(128 // BLOCK):
            low = 8 + block * BLOCK
            u = wind_x[i + 1, block * BLOCK : (block + 1) * BLOCK, :]
            w = wind_y[i, low : low + BLOCK, :]
            for f in range(2):
                here, up, down, right, left = neighbourhood(fields[sweep], f, i, low)
                fields[target][f, i + 1, low : low + BLOCK, :] = (
                    vertical(here) + 0.1 * ((up + down) + (right + left)) - (u * (up - down) + w * (right - left))
                )

    def adjoint_row(sweep, target, i):
        for block in range(128 // BLOCK):
            low = 8 + block * BLOCK
            inner = slice(block * BLOCK, (block + 1) * BLOCK)
            from_down = 0.1 - wind_x[i, inner, :]
            from_up = 0.1 + wind_x[i + 2, inner, :]
            from_left = 0.1 - wind_y[i, low - 1 : low - 1 + BLOCK, :]
            from_right = 0.1 + wind_y[i, low + 1 : low + 1 + BLOCK, :]
            for f in range(2):
                here, up, down, right, left = neighbourhood(fields[sweep], f, i, low)
                fields[target][f, i + 1, low : low + BLOCK, :] = (
                    vertical(here) + (from_down * down + from_up * up) + (from_left * left + from_right * right)
                )

    def each(body, low=0, high=16):
        def step(i, _):
            body(i)
            return 0

        lax.fori_loop(low, high, step, 0)

    for load in loads[:4]:
        load.wait()
    owner = owner_ref[...]
    owner_gx, owner_gy = owner >> 4, owner & 15
    owner_x, owner_y, owner_z = owner_gy >> 2, owner_gx >> 1, ((owner_gy & 3) << 1) | (owner_gx & 1)
    relative = ((owner_y - y + 4) & 3) * 32 + ((owner_x - x + 4) & 3) * 8 + ((owner_z - z + 8) & 7)
    tile_iota = lax.broadcasted_iota(jnp.int32, (128, 512), 0)
    hits = jnp.where(tile_iota == relative, 1.0, 0.0)
    hits_narrow = hits.astype(BF16)
    earlier = jnp.where(
        lax.broadcasted_iota(jnp.int32, (512, 512), 0) < lax.broadcasted_iota(jnp.int32, (512, 512), 1), 1.0, 0.0
    ).astype(BF16)
    slot = jnp.sum(matmul(hits_narrow, earlier) * hits, axis=0, keepdims=True).astype(jnp.int32)
    position = relative * 8 + slot
    column = column_ref[...]
    in_row = tile_iota == (relative & 15) * 8 + slot
    column_high = jnp.where(in_row, (column >> 7).astype(F32), 0.0).astype(BF16)
    column_low = jnp.where(in_row, (column & 127).astype(F32), 0.0).astype(BF16)
    send[:, 16, :] = 128.0 * matmul_nt(hits_narrow, column_high) + matmul_nt(hits_narrow, column_low)
    scale_high, scale_low = split(jnp.broadcast_to(jnp.sqrt(prec_ref[...]), (128, 512)))
    ops_high, ops_low = split(ops[...])

    def pack(chunk, _):
        slots = lax.broadcasted_iota(jnp.int32, (256, 512), 0) + chunk * 256
        pick = jnp.where(slots == position, 1.0, 0.0).astype(BF16)
        scale = matmul_nt(pick, scale_high) + matmul_nt(pick, scale_low)
        rows = matmul(pick, ops_high) + matmul(pick, ops_low)
        target = pl.ds(chunk * GROUP, GROUP)
        send[target, 0:8, :] = (rows[:, :128] * scale).reshape(GROUP, 8, 128)
        send[target, 8:16, :] = (rows[:, 128:] * scale).reshape(GROUP, 8, 128)
        return 0

    lax.fori_loop(0, CHUNKS, pack, 0)

    top_out[...] = jnp.zeros((4, 2, 32, 128), F32)

    loads[4].wait()

    def turn_state(i):
        for f in range(2):
            field_0[f, i + 1, 8:136, :] = flat_native[pl.ds(f * 2048 + i, 128, stride=16), :].T

    each(turn_state)
    pl.semaphore_wait(barrier, 27)
    for step in range(1, 8):
        greet(line_sem, device(x, y, (z + step) & 7))
    first_halo = start_tangent_halo(0)
    pl.semaphore_wait(line_sem, 7)

    pltpu.make_async_copy(send.at[0], recv.at[0], a2a_recv.at[0]).start()

    def dispatch(s, _):
        target = device((x + ((s >> 3) & 3)) & 3, (y + (s >> 5)) & 3, (z + (s & 7)) & 7)
        pltpu.make_async_remote_copy(
            send.at[s], recv.at[s], a2a_send, a2a_recv.at[s >> 5], device_id=target, device_id_type=MESH,
        ).start()
        return 0

    lax.fori_loop(1, 64, dispatch, 0)

    loads[5].wait()
    loads[6].wait()
    wind_x[0] = jnp.full((128, 128), -0.9, F32)
    wind_x[17] = jnp.full((128, 128), 0.9, F32)

    def turn_winds(i):
        wind_x[i + 1] = 0.5 * flat_winds[pl.ds(i, 128, stride=16), :].T
        wind_y[i, 8:136, :] = 0.5 * flat_winds[pl.ds(2048 + i, 128, stride=16), :].T
        wind_y[i, 0:8, :] = jnp.full((8, 128), -0.9, F32)
        wind_y[i, 136:144, :] = jnp.full((8, 128), 0.9, F32)
        rate = jnp.broadcast_to(gamma_ref[pl.ds(i, 1), :], (128, 128)).T
        exchange[i] = jnp.where(lax.broadcasted_iota(jnp.int32, (128, 128), 1) == 0, rate, 0.0)

    each(turn_winds)

    tops = []

    def sweep_rows(sweep, copies, compute, target, meet, after):
        take_lanes(sweep, copies)

        def inside(i):
            compute(i)
            if meet is not None:
                pack_top(meet, 0, target, i)

        each(inside, 1, 15)
        if meet is not None:
            inner = top_copy(meet, 0)
            inner.start()
            tops.append(inner)
            inner.wait_recv()
        each(lambda i: after(i, 0), 1, 15)
        take_rows(sweep, copies)
        for i in (0, 15):
            compute(i)
            if meet is not None:
                pack_top(meet, 1, target, i)
        if meet is not None:
            outer = top_copy(meet, 1)
            outer.start()
            tops.append(outer)
            outer.wait_recv()
        for i in (0, 15):
            after(i, 1)

    sweep_rows(
        0, first_halo, lambda i: tangent_row(0, 1, i), 1, 0, lambda i, part: couple(0, part, 1, i, False)
    )
    second_halo = start_tangent_halo(1)
    lax.fori_loop(64, 128, dispatch, 0)

    def finish_second(i, part):
        couple(1, part, 2, i, False)
        for f in range(2):
            high, low = split(field_2[f, i + 1, 8:136, :])
            second[pl.ds(i * 128, 128), 128 * f : 128 * f + 128] = high
            second[pl.ds(i * 128, 128), 256 + 128 * f : 384 + 128 * f] = low
            field_2[f, i + 1, 8:136, :] = jnp.zeros((128, 128), F32)

    sweep_rows(1, second_halo, lambda i: tangent_row(1, 2, i), 2, 1, finish_second)
    for copy in second_halo:
        copy.wait_send()

    def observe(chunk, _):
        arrived = recv.at[pl.ds(chunk * GROUP, GROUP)]
        pltpu.make_async_copy(arrived, arrived, a2a_recv.at[chunk]).wait()
        group = pl.ds(chunk * GROUP, GROUP)
        where = jnp.concatenate(
            [
                jnp.sum(recv[pl.ds(chunk * GROUP, 16), 16, :], axis=0, keepdims=True),
                jnp.sum(recv[pl.ds(chunk * GROUP + 16, 16), 16, :], axis=0, keepdims=True),
            ],
            axis=1,
        ).astype(jnp.int32)
        down_rows = jnp.broadcast_to(where, (128, 256)).T
        within = lax.broadcasted_iota(jnp.int32, (256, 128), 1)
        for i in range(16):
            pick_cell[:, 128 * i : 128 * i + 128] = jnp.where(down_rows == within + 128 * i, 1.0, 0.0).astype(BF16)
        both = matmul(pick_cell[...], second[...])
        sampled = both[:, :256] + both[:, 256:]
        weights = jnp.concatenate(
            [recv[group, 0:8, :].reshape(256, 128), recv[group, 8:16, :].reshape(256, 128)], axis=1
        )
        spread = jnp.concatenate(split(weights * jnp.sum(sampled * weights, axis=1, keepdims=True)), axis=0)

        def scatter(quarter):
            cell = lax.broadcasted_iota(jnp.int32, (512, 256), 0) + quarter * 512
            pick = jnp.where(cell == where, 1.0, 0.0).astype(BF16)
            added = matmul(jnp.concatenate([pick, pick], axis=1), spread)
            for r in range(4):
                for f in range(2):
                    field_2[f, quarter * 4 + r + 1, 8:136, :] += added[
                        128 * r : 128 * r + 128, 128 * f : 128 * f + 128
                    ]

        each(scatter, 0, 4)
        return 0

    lax.fori_loop(0, CHUNKS, observe, 0)

    def start_adjoint_halo(sweep):
        copies = halo_copies(sweep, (row_out.at[sweep - 2, 0], row_out.at[sweep - 2, 1]))
        for f in range(2):
            row_out[sweep - 2, 0, f] = (0.1 - wind_x[16]) * fields[sweep][f, 16, 8:136, :]
            row_out[sweep - 2, 1, f] = (0.1 + wind_x[1]) * fields[sweep][f, 1, 8:136, :]
        copies[0].start()
        copies[1].start()
        return copies

    def start_adjoint_lanes(sweep, copies):
        right = 0.1 - flat_wind_y[pl.ds(8 + 127, 16, stride=PAD), :]
        left = 0.1 + flat_wind_y[pl.ds(8, 16, stride=PAD), :]
        for f in range(2):
            lane_out[sweep, 0, 16 * f : 16 * f + 16, :] = right * flat_fields[sweep][edge_row(f, 127), :]
            lane_out[sweep, 1, 16 * f : 16 * f + 16, :] = left * flat_fields[sweep][edge_row(f, 0), :]
        copies[2].start()
        copies[3].start()

    for i in (0, 15):
        pack_top(2, 1, 2, i)
    outer_top = top_copy(2, 1)
    outer_top.start()
    each(lambda i: pack_top(2, 0, 2, i), 1, 15)
    inner_top = top_copy(2, 0)
    inner_top.start()
    outer_top.wait_recv()
    for i in (0, 15):
        couple(2, 1, 2, i, True)
    third_halo = start_adjoint_halo(2)
    inner_top.wait_recv()
    each(lambda i: couple(2, 0, 2, i, True), 1, 15)
    start_adjoint_lanes(2, third_halo)
    sweep_rows(2, third_halo, lambda i: adjoint_row(2, 3, i), 3, 3, lambda i, part: couple(3, part, 3, i, True))
    fourth_halo = start_adjoint_halo(3)
    start_adjoint_lanes(3, fourth_halo)

    def turn_back(i, part):
        for f in range(2):
            flat_native[pl.ds(f * 2048 + i, 128, stride=16), :] = field_1[f, i + 1, 8:136, :].T

    sweep_rows(3, fourth_halo, lambda i: adjoint_row(3, 1, i), 1, None, turn_back)
    started = tops + [outer_top, inner_top] + first_halo + third_halo + fourth_halo
    store = pltpu.make_async_copy(native, out_hbm, store_sem)
    store.start()
    for copy in started:
        copy.wait_send()
    sent = recv.at[pl.ds(1, 127)]
    pltpu.make_async_copy(sent, sent, a2a_send).wait()
    store.wait()


def local(state_incr, winds, coupling, background, obs_dest, obs_col, obs_op, obs_prec):
    shape = state_incr.shape[1:]
    tile = (shape[0] * shape[1],) + shape[2:]
    hbm = pl.BlockSpec(memory_space=pltpu.HBM)
    adjoint = pl.pallas_call(
        kernel,
        out_shape=jax.ShapeDtypeStruct(tile, F32),
        in_specs=[hbm] * 7,
        out_specs=pl.BlockSpec(memory_space=pl.ANY),
        scratch_shapes=[
            pltpu.VMEM((1, 512), jnp.int32),
            pltpu.VMEM((1, 512), jnp.int32),
            pltpu.VMEM((1, 512), F32),
            pltpu.VMEM((16, 128), F32),
            pltpu.VMEM(tile, F32),
            pltpu.VMEM(tile, F32),
            pltpu.VMEM((2, 18, PAD, 128), F32),
            pltpu.VMEM((2, 18, PAD, 128), F32),
            pltpu.VMEM((2, 18, PAD, 128), F32),
            pltpu.VMEM((2, 18, PAD, 128), F32),
            pltpu.VMEM((18, 128, 128), F32),
            pltpu.VMEM((16, PAD, 128), F32),
            pltpu.VMEM((16, 128, 128), F32),
            pltpu.VMEM((512, 256), F32),
            pltpu.VMEM((128, 17, 128), F32),
            pltpu.VMEM((128, 17, 128), F32),
            pltpu.VMEM((2, 2, 2, 128, 128), F32),
            pltpu.VMEM((4, 2, 32, 128), F32),
            pltpu.VMEM((4, 2, 32, 128), F32),
            pltpu.VMEM((4, 2, 32, 128), F32),
            pltpu.VMEM((4, 2, 32, 128), F32),
            pltpu.VMEM((2048, 512), BF16),
            pltpu.VMEM((256, 2048), BF16),
            pltpu.SemaphoreType.DMA((7,)),
            pltpu.SemaphoreType.DMA,
            pltpu.SemaphoreType.DMA,
            pltpu.SemaphoreType.DMA((CHUNKS,)),
            pltpu.SemaphoreType.DMA((4, 4)),
            pltpu.SemaphoreType.DMA((4, 4)),
            pltpu.SemaphoreType.DMA((4, 2)),
            pltpu.SemaphoreType.DMA((4, 2)),
            pltpu.SemaphoreType.REGULAR,
        ],
        compiler_params=pltpu.CompilerParams(
            collective_id=0, has_side_effects=True, vmem_limit_bytes=60 * 1024 * 1024
        ),
    )(
        state_incr.reshape(tile), winds.reshape(tile), obs_op,
        obs_dest.reshape(1, -1), obs_col.reshape(1, -1), obs_prec.reshape(1, -1), coupling,
    )
    result = background[0][:, :, None, None] * state_incr[0] + adjoint.reshape(shape)
    return result[None]


def solution(mesh):
    placed = (
        P("comp", None, None, "gx", "gy"),
        P("comp", None, None, "gx", "gy"),
        P("gx", "gy"),
        P("comp", None, None),
        P(("comp", "gx", "gy"), None),
        P(("comp", "gx", "gy")),
        P(("comp", "gx", "gy"), None),
        P(("comp", "gx", "gy")),
    )
    return jax.shard_map(
        local,
        mesh=mesh,
        in_specs=placed,
        out_specs=P("comp", None, None, "gx", "gy"),
        check_vma=False,
    )
```

time: 109 us -> 98 us (0.90)
  Pallas kernels: 102 us -> 94.6 us
  other arithmetic: 5.9 us -> 3.25 us
    pallas_call x1, Pallas kernels: 102 us -> 94.6 us  [local(): pl.pallas_call(kernel, out_shape=jax.ShapeDtypeStruct(tile, F32), in_spec...]
    convert_element_type x2 -> x0, other arithmetic: 1.37 us -> none  [the longest x1 0.68 us: local(): obs_dest[:, 0].astype(F32)]
    another operation x1 -> x0, other arithmetic: 1.29 us -> none  [local(): jnp.stack([obs_dest[:, 0].astype(F32), obs_col.astype(F32), obs_prec])]
where the time goes in v1:
time: 98 us; the launch traced here: 97.9 us
  Pallas kernels  94.6 us (97%)
  other arithmetic  3.25 us (3%)
    pallas_call x1, Pallas kernels, local(): pl.pallas_call(kernel, out_shape=jax.ShapeDtypeStruct(tile, F32), in_spec...  94.6 us
    add x1, other arithmetic, local(): background[0][:, :, None, None] * state_incr[0] + adjoint.reshape(shape)  3.25 us

profile of v1, /device:TPU:1, one launch (start us, length us, event | category | flops | bytes accessed | tf_op | source)
XLA Modules:
  0.0 97.9 jit_solution(9789407085127475699)
XLA Ops:
  0.0 0.0 copy-start
  0.0 0.0 copy-start.1
  0.0 94.6 %shard_map.82 = f32[256,16,128]{2,1,0:T(8,128)} custom-call(f32[256,16,128]{2,1,0:T(8,128)} %bitcast.7, f32[256,16,128]{2,1,0:T(8,128)} %bitcast.9, f32[512,256]{1,0:T(8,128)} %op_hbm.1, s32[1,512]{1,0:T(1,128)} %bitcast.10, s32[1,512]{1,0:T(1,128)} %bitcast.11, f32[1,512]{1,0:T(1,128)} %bitcast.12, f32[16,128]{1,0:T(8,128)} %gamma_hbm.1), custom_call_target="tpu_custom_call" | custom-call | tf_op jit(solution)/shard_map/pallas_call | solution.py:433
  94.6 0.0 copy-done
  94.6 0.0 copy-done.1
  94.7 3.2 %multiply_add_fusion = f32[1,2,128,16,128]{4,3,2,1,0:T(8,128)} fusion(f32[1,2,128,16,128]{4,3,2,1,0:T(8,128)} %bitcast.8, f32[1,2,128,16,128]{4,3,2,1,0:T(8,128)S(1)} %copy-done, f32[2,128]{1,0:T(2,128)S(1)} %bitcast.13), kind=kLoop, calls=%fused_computation | loop fusion | flops 1048576 | bytes 6292480 | tf_op jit(solution)/shard_map/add | solution.py:479
Async XLA Ops:
  0.0 94.6 %copy-start = (f32[1,2,128,16,128]{4,3,2,1,0:T(8,128)S(1)}, f32[1,2,128,16,128]{4,3,2,1,0:T(8,128)}, u32[]{:S(2)}) copy-start(f32[1,2,128,16,128]{4,3,2,1,0:T(8,128)} %param.8) | copy-start | bytes 6291460
  0.0 94.6 %copy-start.1 = (f32[1,2,128]{2,1,0:T(2,128)S(1)}, f32[1,2,128]{2,1,0:T(2,128)}, u32[]{:S(2)}) copy-start(f32[1,2,128]{2,1,0:T(2,128)} %param.11) | copy-start | bytes 3076

commit v2 on v1

--- a/solution.py
+++ b/solution.py
@@ -87,8 +87,8 @@
     flat_winds = native_winds.reshape(4096, 128)
     flat_wind_y = wind_y.reshape(16 * PAD, 128)
 
-    def edge_row(f, j):
-        return pl.ds((f * 18 + 1) * PAD + 8 + j, 16, stride=PAD)
+    def edge_row(f, j, first=0, count=16):
+        return pl.ds((f * 18 + 1 + first) * PAD + 8 + j, count, stride=PAD)
 
     def halo_copies(sweep, sources):
         pairs = (
@@ -109,21 +109,22 @@
         copies = halo_copies(
             sweep, (fields[sweep].at[:, 16, pl.ds(8, 128), :], fields[sweep].at[:, 1, pl.ds(8, 128), :])
         )
-        copies[0].start()
-        copies[1].start()
         for f in range(2):
             lane_out[sweep, 0, 16 * f : 16 * f + 16, :] = flat_fields[sweep][edge_row(f, 127), :]
             lane_out[sweep, 1, 16 * f : 16 * f + 16, :] = flat_fields[sweep][edge_row(f, 0), :]
-        copies[2].start()
-        copies[3].start()
+        for copy in copies[2:] + copies[:2]:
+            copy.start()
         return copies
 
-    def take_lanes(sweep, copies):
-        copies[2].wait_recv()
-        copies[3].wait_recv()
-        for f in range(2):
-            flat_fields[sweep][edge_row(f, -1), :] = lane_in[sweep, 0, 16 * f : 16 * f + 16, :] * has_left
-            flat_fields[sweep][edge_row(f, 128), :] = lane_in[sweep, 1, 16 * f : 16 * f + 16, :] * has_right
+    def add_lanes(sweep, target, first, count):
+        for f in range(2):
+            for side, j, present in ((0, 0, has_left), (1, 127, has_right)):
+                arrived = lane_in[sweep, side, 16 * f + first : 16 * f + first + count, :] * present
+                if sweep < 2:
+                    w = flat_wind_y[pl.ds(first * PAD + 8 + j, count, stride=PAD), :]
+                    arrived = arrived * (0.1 + w if side == 0 else 0.1 - w)
+                rows = edge_row(f, j, first, count)
+                flat_fields[target][rows, :] = flat_fields[target][rows, :] + arrived
 
     def take_rows(sweep, copies):
         copies[0].wait_recv()
@@ -137,12 +138,12 @@
         def _():
             fields[sweep][:, 17, 8:136, :] = jnp.zeros((2, 128, 128), F32)
 
-    def pack_top(sweep, part, field, i):
+    def pack_top(sweep, part, field, i, blocks=range(16)):
         for f in range(2):
             rows = pl.ds(f * 16 + (i >> 3) * 8, 8)
             packed = top_out[sweep, part, rows, :]
             base = (i & 7) * 16
-            for n in range(16):
+            for n in blocks:
                 level = fields[field][f, i + 1, 8 + 8 * n : 16 + 8 * n, 0:1]
                 packed = jnp.where(lane_8 == base + n, jnp.broadcast_to(level, (8, 128)), packed)
             top_out[sweep, part, rows, :] = packed
@@ -153,22 +154,22 @@
             device_id=partner, device_id_type=MESH,
         )
 
-    def couple(sweep, part, field, i, transposed):
+    def couple(sweep, part, field, i, transposed, runs=((0, 8), (8, 16))):
         for f in range(2):
             rows = pl.ds(f * 16 + (i >> 3) * 8, 8)
             packed = pltpu.roll(top_in[sweep, part, rows, :], (128 - (i & 7) * 16) & 127, 1)
-            for half in range(2):
-                low = 8 + 64 * half
-                own = fields[field][f, i + 1, low : low + 64, :]
+            for first, last in runs:
+                inner = slice(8 + 8 * first, 8 + 8 * last)
+                own = fields[field][f, i + 1, inner, :]
                 peer = jnp.concatenate(
-                    [packed if n == 0 else pltpu.roll(packed, 128 - n, 1) for n in range(8 * half, 8 * half + 8)], axis=0
+                    [packed if n == 0 else pltpu.roll(packed, 128 - n, 1) for n in range(first, last)], axis=0
                 )
-                rate = exchange[i, 64 * half : 64 * half + 64, :]
+                rate = exchange[i, 8 * first : 8 * last, :]
                 if transposed:
                     value = own - rate * (own_share * own - peer_share * peer)
                 else:
                     value = own - rate * (own_share * (own - peer))
-                fields[field][f, i + 1, low : low + 64, :] = value
+                fields[field][f, i + 1, inner, :] = value
 
     def vertical(here):
         above = jnp.where(lane == 127, here, pltpu.roll(here, 127, 1))
@@ -250,6 +251,10 @@
     lax.fori_loop(0, CHUNKS, pack, 0)
 
     top_out[...] = jnp.zeros((4, 2, 32, 128), F32)
+    for flat in flat_fields:
+        for f in range(2):
+            for j in (-1, 128):
+                flat[edge_row(f, j), :] = jnp.zeros((16, 128), F32)
 
     loads[4].wait()
 
@@ -257,10 +262,10 @@
         for f in range(2):
             field_0[f, i + 1, 8:136, :] = flat_native[pl.ds(f * 2048 + i, 128, stride=16), :].T
 
-    each(turn_state)
     pl.semaphore_wait(barrier, 27)
     for step in range(1, 8):
         greet(line_sem, device(x, y, (z + step) & 7))
+    each(turn_state)
     first_halo = start_tangent_halo(0)
     pl.semaphore_wait(line_sem, 7)
 
@@ -293,15 +298,12 @@
     tops = []
 
     def sweep_rows(sweep, copies, compute, target, meet, after):
-        take_lanes(sweep, copies)
-
-        def inside(i):
-            compute(i)
-            if meet is not None:
-                pack_top(meet, 0, target, i)
-
-        each(inside, 1, 15)
+        each(compute, 1, 15)
+        copies[2].wait_recv()
+        copies[3].wait_recv()
+        add_lanes(sweep, target, 0, 16)
         if meet is not None:
+            each(lambda i: pack_top(meet, 0, target, i), 1, 15)
             inner = top_copy(meet, 0)
             inner.start()
             tops.append(inner)
@@ -310,6 +312,7 @@
         take_rows(sweep, copies)
         for i in (0, 15):
             compute(i)
+            add_lanes(sweep, target, i, 1)
             if meet is not None:
                 pack_top(meet, 1, target, i)
         if meet is not None:
@@ -377,14 +380,6 @@
 
     def start_adjoint_halo(sweep):
         copies = halo_copies(sweep, (row_out.at[sweep - 2, 0], row_out.at[sweep - 2, 1]))
-        for f in range(2):
-            row_out[sweep - 2, 0, f] = (0.1 - wind_x[16]) * fields[sweep][f, 16, 8:136, :]
-            row_out[sweep - 2, 1, f] = (0.1 + wind_x[1]) * fields[sweep][f, 1, 8:136, :]
-        copies[0].start()
-        copies[1].start()
-        return copies
-
-    def start_adjoint_lanes(sweep, copies):
         right = 0.1 - flat_wind_y[pl.ds(8 + 127, 16, stride=PAD), :]
         left = 0.1 + flat_wind_y[pl.ds(8, 16, stride=PAD), :]
         for f in range(2):
@@ -392,24 +387,31 @@
             lane_out[sweep, 1, 16 * f : 16 * f + 16, :] = left * flat_fields[sweep][edge_row(f, 0), :]
         copies[2].start()
         copies[3].start()
+        for f in range(2):
+            row_out[sweep - 2, 0, f] = (0.1 - wind_x[16]) * fields[sweep][f, 16, 8:136, :]
+        copies[0].start()
+        for f in range(2):
+            row_out[sweep - 2, 1, f] = (0.1 + wind_x[1]) * fields[sweep][f, 1, 8:136, :]
+        copies[1].start()
+        return copies
 
     for i in (0, 15):
         pack_top(2, 1, 2, i)
+    each(lambda i: pack_top(2, 1, 2, i, (0, 15)), 1, 15)
     outer_top = top_copy(2, 1)
     outer_top.start()
-    each(lambda i: pack_top(2, 0, 2, i), 1, 15)
+    each(lambda i: pack_top(2, 0, 2, i, range(1, 15)), 1, 15)
     inner_top = top_copy(2, 0)
     inner_top.start()
     outer_top.wait_recv()
     for i in (0, 15):
         couple(2, 1, 2, i, True)
+    each(lambda i: couple(2, 1, 2, i, True, ((0, 1), (15, 16))), 1, 15)
     third_halo = start_adjoint_halo(2)
     inner_top.wait_recv()
-    each(lambda i: couple(2, 0, 2, i, True), 1, 15)
-    start_adjoint_lanes(2, third_halo)
+    each(lambda i: couple(2, 0, 2, i, True, ((1, 8), (8, 15))), 1, 15)
     sweep_rows(2, third_halo, lambda i: adjoint_row(2, 3, i), 3, 3, lambda i, part: couple(3, part, 3, i, True))
     fourth_halo = start_adjoint_halo(3)
-    start_adjoint_lanes(3, fourth_halo)
 
     def turn_back(i, part):
         for f in range(2):

time: 98 us -> 84 us (0.86)
  Pallas kernels: 94.6 us -> 80.4 us
    pallas_call x1, Pallas kernels: 94.6 us -> 80.4 us  [local(): pl.pallas_call(kernel, out_shape=jax.ShapeDtypeStruct(tile, F32), in_spec...]
where the time goes in v2:
time: 84 us; the launch traced here: 83.7 us
  Pallas kernels  80.4 us (96%)
  other arithmetic  3.25 us (4%)
    pallas_call x1, Pallas kernels, local(): pl.pallas_call(kernel, out_shape=jax.ShapeDtypeStruct(tile, F32), in_spec...  80.4 us
    add x1, other arithmetic, local(): background[0][:, :, None, None] * state_incr[0] + adjoint.reshape(shape)  3.25 us

profile of v2, /device:TPU:1, one launch (start us, length us, event | category | flops | bytes accessed | tf_op | source)
XLA Modules:
  0.0 83.7 jit_solution(14045474629535878218)
XLA Ops:
  0.0 0.0 copy-start
  0.0 0.0 copy-start.1
  0.0 80.4 %shard_map.82 = f32[256,16,128]{2,1,0:T(8,128)} custom-call(f32[256,16,128]{2,1,0:T(8,128)} %bitcast.7, f32[256,16,128]{2,1,0:T(8,128)} %bitcast.9, f32[512,256]{1,0:T(8,128)} %op_hbm.1, s32[1,512]{1,0:T(1,128)} %bitcast.10, s32[1,512]{1,0:T(1,128)} %bitcast.11, f32[1,512]{1,0:T(1,128)} %bitcast.12, f32[16,128]{1,0:T(8,128)} %gamma_hbm.1), custom_call_target="tpu_custom_call" | custom-call | tf_op jit(solution)/shard_map/pallas_call | solution.py:435
  80.4 0.0 copy-done
  80.4 0.0 copy-done.1
  80.4 3.2 %multiply_add_fusion = f32[1,2,128,16,128]{4,3,2,1,0:T(8,128)} fusion(f32[1,2,128,16,128]{4,3,2,1,0:T(8,128)} %bitcast.8, f32[1,2,128,16,128]{4,3,2,1,0:T(8,128)S(1)} %copy-done, f32[2,128]{1,0:T(2,128)S(1)} %bitcast.13), kind=kLoop, calls=%fused_computation | loop fusion | flops 1048576 | bytes 6292480 | tf_op jit(solution)/shard_map/add | solution.py:481
Async XLA Ops:
  0.0 80.4 %copy-start = (f32[1,2,128,16,128]{4,3,2,1,0:T(8,128)S(1)}, f32[1,2,128,16,128]{4,3,2,1,0:T(8,128)}, u32[]{:S(2)}) copy-start(f32[1,2,128,16,128]{4,3,2,1,0:T(8,128)} %param.8) | copy-start | bytes 6291460
  0.0 80.4 %copy-start.1 = (f32[1,2,128]{2,1,0:T(2,128)S(1)}, f32[1,2,128]{2,1,0:T(2,128)}, u32[]{:S(2)}) copy-start(f32[1,2,128]{2,1,0:T(2,128)} %param.11) | copy-start | bytes 3076

commit v3 on v2

--- a/solution.py
+++ b/solution.py
@@ -32,11 +32,11 @@
 
 
 def kernel(
-    state_hbm, winds_hbm, op_hbm, owner_hbm, column_hbm, prec_hbm, gamma_hbm, out_hbm,
-    owner_ref, column_ref, prec_ref, gamma_ref, native, native_winds, field_0, field_1, field_2, field_3, wind_x, wind_y, exchange, ops, send, recv,
+    state_hbm, winds_hbm, op_hbm, owner_hbm, column_hbm, prec_hbm, gamma_hbm, precision_hbm, out_ref,
+    owner_ref, column_ref, prec_ref, gamma_ref, precision_ref, native, native_winds, field_0, field_1, field_2, field_3, wind_x, wind_y, exchange, ops, send, recv,
     row_out, lane_out, lane_in, top_out, top_in,
     second, pick_cell,
-    load_sem, store_sem, a2a_send, a2a_recv, halo_send, halo_recv, top_send, top_recv, line_sem,
+    load_sem, a2a_send, a2a_recv, halo_send, halo_recv, top_send, top_recv, line_sem,
 ):
     comp = lax.axis_index("comp")
     gx = lax.axis_index("gx")
@@ -48,7 +48,7 @@
         for n, (src, dst) in enumerate(
             (
                 (owner_hbm, owner_ref), (column_hbm, column_ref), (prec_hbm, prec_ref), (op_hbm, ops),
-                (state_hbm, native), (winds_hbm, native_winds), (gamma_hbm, gamma_ref),
+                (state_hbm, native), (winds_hbm, native_winds), (gamma_hbm, gamma_ref), (precision_hbm, precision_ref),
             )
         )
     ]
@@ -84,6 +84,7 @@
     fields = (field_0, field_1, field_2, field_3)
     flat_fields = [field.reshape(2 * 18 * PAD, 128) for field in fields]
     flat_native = native.reshape(4096, 128)
+    flat_out = out_ref.reshape(4096, 128)
     flat_winds = native_winds.reshape(4096, 128)
     flat_wind_y = wind_y.reshape(16 * PAD, 128)
 
@@ -214,7 +215,7 @@
             body(i)
             return 0
 
-        lax.fori_loop(low, high, step, 0)
+        lax.fori_loop(low, high, step, 0, unroll=2)
 
     for load in loads[:4]:
         load.wait()
@@ -278,10 +279,11 @@
         ).start()
         return 0
 
-    lax.fori_loop(1, 64, dispatch, 0)
+    lax.fori_loop(1, 32, dispatch, 0)
 
     loads[5].wait()
     loads[6].wait()
+    loads[7].wait()
     wind_x[0] = jnp.full((128, 128), -0.9, F32)
     wind_x[17] = jnp.full((128, 128), 0.9, F32)
 
@@ -323,11 +325,19 @@
         for i in (0, 15):
             after(i, 1)
 
+    precision = [jnp.broadcast_to(precision_ref[f : f + 1, :], (128, 128)).T for f in range(2)]
+
+    def scale_state(i):
+        for f in range(2):
+            rows = pl.ds(f * 2048 + i, 128, stride=16)
+            flat_out[rows, :] = precision[f] * flat_native[rows, :]
+
+    each(scale_state)
     sweep_rows(
         0, first_halo, lambda i: tangent_row(0, 1, i), 1, 0, lambda i, part: couple(0, part, 1, i, False)
     )
     second_halo = start_tangent_halo(1)
-    lax.fori_loop(64, 128, dispatch, 0)
+    lax.fori_loop(32, 128, dispatch, 0)
 
     def finish_second(i, part):
         couple(1, part, 2, i, False)
@@ -415,33 +425,32 @@
 
     def turn_back(i, part):
         for f in range(2):
-            flat_native[pl.ds(f * 2048 + i, 128, stride=16), :] = field_1[f, i + 1, 8:136, :].T
+            rows = pl.ds(f * 2048 + i, 128, stride=16)
+            flat_out[rows, :] = flat_out[rows, :] + field_1[f, i + 1, 8:136, :].T
 
     sweep_rows(3, fourth_halo, lambda i: adjoint_row(3, 1, i), 1, None, turn_back)
     started = tops + [outer_top, inner_top] + first_halo + third_halo + fourth_halo
-    store = pltpu.make_async_copy(native, out_hbm, store_sem)
-    store.start()
     for copy in started:
         copy.wait_send()
     sent = recv.at[pl.ds(1, 127)]
     pltpu.make_async_copy(sent, sent, a2a_send).wait()
-    store.wait()
 
 
 def local(state_incr, winds, coupling, background, obs_dest, obs_col, obs_op, obs_prec):
     shape = state_incr.shape[1:]
     tile = (shape[0] * shape[1],) + shape[2:]
     hbm = pl.BlockSpec(memory_space=pltpu.HBM)
-    adjoint = pl.pallas_call(
+    result = pl.pallas_call(
         kernel,
-        out_shape=jax.ShapeDtypeStruct(tile, F32),
-        in_specs=[hbm] * 7,
-        out_specs=pl.BlockSpec(memory_space=pl.ANY),
+        out_shape=pltpu.VMEM(tile, F32),
+        in_specs=[hbm] * 8,
+        out_specs=pl.BlockSpec(memory_space=pltpu.VMEM),
         scratch_shapes=[
             pltpu.VMEM((1, 512), jnp.int32),
             pltpu.VMEM((1, 512), jnp.int32),
             pltpu.VMEM((1, 512), F32),
             pltpu.VMEM((16, 128), F32),
+            pltpu.VMEM((2, 128), F32),
             pltpu.VMEM(tile, F32),
             pltpu.VMEM(tile, F32),
             pltpu.VMEM((2, 18, PAD, 128), F32),
@@ -461,8 +470,7 @@
             pltpu.VMEM((4, 2, 32, 128), F32),
             pltpu.VMEM((2048, 512), BF16),
             pltpu.VMEM((256, 2048), BF16),
-            pltpu.SemaphoreType.DMA((7,)),
-            pltpu.SemaphoreType.DMA,
+            pltpu.SemaphoreType.DMA((8,)),
             pltpu.SemaphoreType.DMA,
             pltpu.SemaphoreType.DMA((CHUNKS,)),
             pltpu.SemaphoreType.DMA((4, 4)),
@@ -476,10 +484,9 @@
         ),
     )(
         state_incr.reshape(tile), winds.reshape(tile), obs_op,
-        obs_dest.reshape(1, -1), obs_col.reshape(1, -1), obs_prec.reshape(1, -1), coupling,
+        obs_dest.reshape(1, -1), obs_col.reshape(1, -1), obs_prec.reshape(1, -1), coupling, background[0],
     )
-    result = background[0][:, :, None, None] * state_incr[0] + adjoint.reshape(shape)
-    return result[None]
+    return result.reshape((1,) + shape)
 
 
 def solution(mesh):

time: 84 us -> 78.4 us (0.933)
  Pallas kernels: 80.4 us -> 76.8 us
  other arithmetic: 3.25 us -> 0 us
  local copies, waits for them, and re-layouts: 0.01 us -> 1.32 us
    pallas_call x1, Pallas kernels: 80.4 us -> 76.8 us  [local(): pl.pallas_call(kernel, out_shape=pltpu.VMEM(tile, F32), in_specs=[hbm] *...]
    add x1 -> x0, other arithmetic: 3.25 us -> none  [local(): background[0][:, :, None, None] * state_incr[0] + adjoint.reshape(shape)]
    unnamed x4 -> x1, local copies, waits for them, and re-layouts: 0.01 us -> 1.32 us
where the time goes in v3:
time: 78.4 us; the launch traced here: 78.1 us
  Pallas kernels  76.8 us (98%)
  local copies, waits for them, and re-layouts  1.32 us (2%)
    pallas_call x1, Pallas kernels, local(): pl.pallas_call(kernel, out_shape=pltpu.VMEM(tile, F32), in_specs=[hbm] *...  76.8 us

profile of v3, /device:TPU:1, one launch (start us, length us, event | category | flops | bytes accessed | tf_op | source)
XLA Modules:
  0.0 78.1 jit_solution(447107662188913174)
XLA Ops:
  0.0 76.8 %shard_map.82 = f32[256,16,128]{2,1,0:T(8,128)S(1)} custom-call(f32[256,16,128]{2,1,0:T(8,128)} %bitcast.8, f32[256,16,128]{2,1,0:T(8,128)} %bitcast.9, f32[512,256]{1,0:T(8,128)} %op_hbm.1, s32[1,512]{1,0:T(1,128)} %bitcast.10, s32[1,512]{1,0:T(1,128)} %bitcast.11, f32[1,512]{1,0:T(1,128)} %bitcast.12, f32[16,128]{1,0:T(8,128)} %gamma_hbm.1, f32[2,128]{1,0:T(2,128)} %bitcast.13), custom_call_target="tpu_custom_call" | custom-call | tf_op jit(solution)/shard_map/pallas_call | solution.py:443
  76.8 1.3 %copy.10 = f32[1,2,128,16,128]{4,3,2,1,0:T(8,128)} copy(f32[1,2,128,16,128]{4,3,2,1,0:T(8,128)S(1)} %bitcast.7) | data formatting | bytes 4194304

commit v4 on v3

--- a/solution.py
+++ b/solution.py
@@ -67,13 +67,13 @@
     def greet(semaphore, target):
         pl.semaphore_signal(semaphore, inc=1, device_id=target, device_id_type=MESH)
 
-    for target in neighbours:
-        greet(barrier, target)
-    greet(barrier, partner)
     for step in range(1, 8):
         greet(barrier, device(x, y, (z + step) & 7))
     for step in range(1, 16):
         greet(barrier, device((x + step) & 3, (y + step // 4) & 3, z))
+    for target in neighbours:
+        greet(barrier, target)
+    greet(barrier, partner)
 
     lane = lax.broadcasted_iota(jnp.int32, (BLOCK, 128), 1)
     lane_8 = lax.broadcasted_iota(jnp.int32, (8, 128), 1)
@@ -215,7 +215,7 @@
             body(i)
             return 0
 
-        lax.fori_loop(low, high, step, 0, unroll=2)
+        lax.fori_loop(low, high, step, 0, unroll=4 if (high - low) % 4 == 0 else 7)
 
     for load in loads[:4]:
         load.wait()
@@ -337,7 +337,7 @@
         0, first_halo, lambda i: tangent_row(0, 1, i), 1, 0, lambda i, part: couple(0, part, 1, i, False)
     )
     second_halo = start_tangent_halo(1)
-    lax.fori_loop(32, 128, dispatch, 0)
+    lax.fori_loop(32, 128, dispatch, 0, unroll=4)
 
     def finish_second(i, part):
         couple(1, part, 2, i, False)

time: 78.4 us -> 77.8 us (level)
  no operation moved by 1% of the time
where the time goes in v4:
time: 77.8 us; the launch traced here: 77.7 us
  Pallas kernels  76.4 us (98%)
  local copies, waits for them, and re-layouts  1.32 us (2%)
    pallas_call x1, Pallas kernels, local(): pl.pallas_call(kernel, out_shape=pltpu.VMEM(tile, F32), in_specs=[hbm] *...  76.4 us

profile of v4, /device:TPU:1, one launch (start us, length us, event | category | flops | bytes accessed | tf_op | source)
XLA Modules:
  0.0 77.7 jit_solution(15823773883707118476)
XLA Ops:
  0.0 76.4 %shard_map.82 = f32[256,16,128]{2,1,0:T(8,128)S(1)} custom-call(f32[256,16,128]{2,1,0:T(8,128)} %bitcast.8, f32[256,16,128]{2,1,0:T(8,128)} %bitcast.9, f32[512,256]{1,0:T(8,128)} %op_hbm.1, s32[1,512]{1,0:T(1,128)} %bitcast.10, s32[1,512]{1,0:T(1,128)} %bitcast.11, f32[1,512]{1,0:T(1,128)} %bitcast.12, f32[16,128]{1,0:T(8,128)} %gamma_hbm.1, f32[2,128]{1,0:T(2,128)} %bitcast.13), custom_call_target="tpu_custom_call" | custom-call | tf_op jit(solution)/shard_map/pallas_call | solution.py:443
  76.4 1.3 %copy.10 = f32[1,2,128,16,128]{4,3,2,1,0:T(8,128)} copy(f32[1,2,128,16,128]{4,3,2,1,0:T(8,128)S(1)} %bitcast.7) | data formatting | bytes 4194304
